TPU v7x, 32 devices: a whole 2x2x4 slice. The times are simulated.
32 devices in a mesh: srv: 8 (over y, x, core), head: 4 (over z).
Axes of the slice: x: 2, y: 2, z: 4, core: 2. Of those that a mesh axis runs over, the one named last changes fastest.
Arguments:
- queries: bfloat16 [2048, 8192], P('srv', 'head'), may hold values from -200 to 200
- key_value_pair: bfloat16 [2, 2048, 1024], P(None, 'srv', 'head'), may hold values from -200 to 200
- lengths: int32 [8], replicated, may hold values from 1 to 1024, 2048 in all
Outputs:
- attended: bfloat16 [2048, 8192], P(('srv', 'head'))
All inputs are finite; a program needn't handle non-finite values.
Results may differ from a plain program's by a relative error of at most 0.012.
Values may be sent and summed in bfloat16 or wider, within the bound.
A program may use at most 64 MiB of HBM per device.

v0:
```python
import math
import jax
import jax.numpy as jnp
from jax import lax
from jax.sharding import PartitionSpec as P

HEAD_SIZE = 128


def doc_start(doc_lengths, row_ids):
    doc_ends = jnp.cumsum(doc_lengths)
    passed = doc_ends[None, :] <= row_ids[:, None]
    return jnp.max(jnp.where(passed, doc_ends[None, :], 0), axis=1)


def apply_rotary(vectors, positions):
    half_width = vectors.shape[-1] // 2
    steps_up = jnp.arange(half_width, dtype=jnp.float32) * (2.0 / vectors.shape[-1])
    inverse = jnp.exp(-steps_up * math.log(500000.0))
    angles = positions[:, None] * inverse[None, :]
    cosine = jnp.cos(angles)[:, None, :]
    sine_table = jnp.sin(angles)[:, None, :]
    low_half = vectors[..., :half_width]
    high_half = vectors[..., half_width:]
    return jnp.concatenate(
        [low_half * cosine - high_half * sine_table, high_half * cosine + low_half * sine_table],
        axis=-1,
    )


def merge_shard(state, query_group, row_group, start_group, key_rows, value_rows, key_ids):
    run_max, run_total, run_acc = state
    group_rows, kv_local, per_kv, head_width = query_group.shape
    all_heads = kv_local * per_kv
    scores = jnp.einsum(
        "rhgd,khd->hgrk", query_group, key_rows, preferred_element_type=jnp.float32
    ) * HEAD_SIZE ** (-0.5)
    allowed = (
        (key_ids[None, :] <= row_group[:, None]) & (key_ids[None, :] >= start_group[:, None])
    )[None, None]
    masked = jnp.where(allowed, scores, -1e30)
    shard_max = jnp.max(masked, axis=3)
    weights = jnp.where(allowed, jnp.exp(masked - shard_max[..., None]), 0.0)
    shard_total = jnp.sum(weights, axis=3)
    part_value = jnp.einsum(
        "hgrk,khd->rhgd",
        weights.astype(jnp.bfloat16),
        value_rows,
        preferred_element_type=jnp.float32,
    ).reshape(group_rows, all_heads, head_width)
    shard_max = jnp.transpose(shard_max, (2, 0, 1)).reshape(group_rows, all_heads)
    shard_total = jnp.transpose(shard_total, (2, 0, 1)).reshape(group_rows, all_heads)
    new_max = jnp.maximum(run_max, shard_max)
    old_factor = jnp.exp(run_max - new_max)
    new_factor = jnp.exp(shard_max - new_max)
    new_total = run_total * old_factor + shard_total * new_factor
    new_acc = run_acc * old_factor[..., None] + part_value * new_factor[..., None]
    return (new_max, new_total, new_acc)


def attend(query_flat, row_ids, starts, packed_pair, shard_rows, kv_local):
    total_rows, query_width = query_flat.shape
    all_heads = query_width // HEAD_SIZE
    per_kv = all_heads // kv_local
    group_rows = min(total_rows, 64)
    group_count = total_rows // group_rows
    query_view = query_flat.reshape(total_rows, kv_local, per_kv, HEAD_SIZE)

    def add_shard(state, kv_shard, key_low):
        kv_view = kv_shard.reshape(shard_rows, 2, kv_local, HEAD_SIZE)
        key_rows = kv_view[:, 0]
        value_rows = kv_view[:, 1]
        key_ids = key_low + jnp.arange(shard_rows, dtype=jnp.int32)
        key_high = key_low + shard_rows - 1
        updated = []
        for group_index in range(group_count):
            row_slice = slice(group_index * group_rows, (group_index + 1) * group_rows)
            group_state = (state[0][row_slice], state[1][row_slice], state[2][row_slice])
            needed = jnp.any((starts[row_slice] <= key_high) & (row_ids[row_slice] >= key_low))
            group_state = lax.cond(
                needed,
                lambda current, row_slice=row_slice: merge_shard(
                    current,
                    query_view[row_slice],
                    row_ids[row_slice],
                    starts[row_slice],
                    key_rows,
                    value_rows,
                    key_ids,
                ),
                lambda current: current,
                group_state,
            )
            updated.append(group_state)
        return (
            jnp.concatenate([item[0] for item in updated], axis=0),
            jnp.concatenate([item[1] for item in updated], axis=0),
            jnp.concatenate([item[2] for item in updated], axis=0),
        )

    initial = (
        jnp.full((total_rows, all_heads), -1e30, jnp.float32),
        jnp.zeros((total_rows, all_heads), jnp.float32),
        jnp.zeros((total_rows, all_heads, HEAD_SIZE), jnp.float32),
    )
    running = initial
    kv_piece = lax.all_gather(packed_pair, "srv", axis=0, tiled=True)
    shard_count = kv_piece.shape[0] // shard_rows
    shards = kv_piece.reshape(shard_count, shard_rows, kv_piece.shape[1])

    def one_step(current, packed):
        kv_shard, shard_index = packed
        return (add_shard(current, kv_shard, shard_index * shard_rows), None)

    running, _ = lax.scan(one_step, running, (shards, jnp.arange(shard_count, dtype=jnp.int32)))
    run_max, run_total, run_acc = running
    return (run_acc / run_total[..., None]).reshape(total_rows, query_width).astype(jnp.bfloat16)


def body(queries, key_value_pair, lengths):
    tok_rows = queries.shape[0]
    query_width = queries.shape[1]
    all_heads = query_width // HEAD_SIZE
    kv_local = key_value_pair.shape[2] // HEAD_SIZE
    own_index = lax.axis_index("srv")
    local_ids = jnp.arange(tok_rows, dtype=jnp.int32)
    row_ids = own_index * tok_rows + local_ids
    starts = doc_start(lengths, row_ids)
    positions = (row_ids - starts).astype(jnp.float32)
    query_rotated = apply_rotary(
        queries.reshape(tok_rows, all_heads, HEAD_SIZE).astype(jnp.float32), positions
    ).astype(jnp.bfloat16)
    key_rotated = apply_rotary(
        key_value_pair[0].reshape(tok_rows, kv_local, HEAD_SIZE).astype(jnp.float32), positions
    ).astype(jnp.bfloat16)
    packed_pair = jnp.stack(
        [key_rotated, key_value_pair[1].reshape(tok_rows, kv_local, HEAD_SIZE)], axis=1
    )
    packed_pair = packed_pair.reshape(tok_rows, 2 * kv_local * HEAD_SIZE)
    query_flat = query_rotated.reshape(tok_rows, query_width)
    result = attend(query_flat, row_ids, starts, packed_pair, tok_rows, kv_local)
    return lax.all_to_all(result, "head", split_axis=0, concat_axis=1, tiled=True)


def solution(mesh):
    in_specs = (P("srv", "head"), P(None, "srv", "head"), P())
    out_specs = P(("srv", "head"), None)
    return jax.shard_map(body, mesh=mesh, in_specs=in_specs, out_specs=out_specs, check_vma=False)
```

profile of v0, /device:TPU:6, one launch (start us, length us, event | category | flops | bytes accessed | tf_op | source)
XLA Modules:
  0.0 184.0 jit_solution(17758708910333524287)
XLA Ops:
  6.6 0.9 reduce-window.8
  7.6 1.0 slice_convert_fusion
  9.2 0.7 pad_maximum_fusion.4
  11.4 1.4 subtract_convert_fusion
  13.4 25.0 %all-gather.2.cloned.1.call-done = bf16[2048,512]{0,1:T(8,128)(2,1)} async-done(((bf16[256,512]{0,1:T(8,128)(2,1)}), bf16[2048,512]{0,1:T(8,128)(2,1)}) %all-gather.2.cloned.1.call-update) | async-done | bytes 2097168 | tf_op jit(solution)/shard_map/all_gather | solution.py:107
  38.4 3.9 %copy.46 = bf16[2048,512]{1,0:T(8,128)(2,1)} copy(bf16[2048,512]{0,1:T(8,128)(2,1)} %all-gather.2.cloned.1.call-done) | data formatting | bytes 4194304 | tf_op jit(solution)/shard_map/all_gather | solution.py:107
  42.4 1.5 broadcast_in_dim.125
  43.9 108.8 %while.18 = (s32[]{:T(128)}, f32[256,16]{0,1:T(8,128)S(1)}, f32[256,16]{0,1:T(8,128)S(1)}, f32[256,16,128]{2,0,1:T(8,128)}, s32[256]{0:T(256)S(1)}, /*index=5*/s...) while((s32[]{:T(128)}, f32[256,16]{0,1:T(8,128)S(1)}, ...), condition=%wide.region_23.24_spmd, body=%wide.region_2.23_spmd.sunk | while | flops 549692672 | bytes 33666752 | solution.py:115
  45.2 1.0 constant_dynamic-slice_fusion.2
  46.4 1.7 fusion.81
  48.0 0.7 and_reduce_fusion.5
  51.2 1.4 pad_maximum_fusion.10
  54.1 1.0 constant_dynamic-slice_fusion.2
  55.3 1.7 fusion.81
  57.0 0.7 and_reduce_fusion.5
  60.2 1.4 pad_maximum_fusion.10
  63.1 1.0 constant_dynamic-slice_fusion.2
  64.2 1.7 fusion.81
  65.9 0.7 and_reduce_fusion.5
  67.3 1.8 conditional.11
  69.6 1.9 %conditional.10 = ((f32[64,16]{0,1:T(8,128)S(1)}, f32[64,16]{0,1:T(8,128)S(1)}, f32[64,16,128]{2,0,1:T(8,128)S(1)})) conditional(s32[]{:T(128)} %convert_element_type.111, (f32[64,16]{0,1:T(8,128)S(1)}, f32[64,16]{0,1:T(8,128)S(1)}, f32[64,16,128]{2,0,1:T(8,128)S(1)}) %tuple.134, (s32[256]{0:T(256)S(1)}, s32[256]{0:T(256)S(1)}, s32[256]{0:T(256)S(1)}, ...), branch_computations={%region_9.9_spmd, %region_10.12_spmd} | conditional | flops 137023488 | bytes 5892640 | solution.py:80
  72.2 1.8 conditional.9
  74.6 1.9 %conditional.8 = ((f32[64,16]{0,1:T(8,128)S(1)}, f32[64,16]{0,1:T(8,128)S(1)}, f32[64,16,128]{2,0,1:T(8,128)S(1)})) conditional(s32[]{:T(128)} %convert_element_type.109, (f32[64,16]{0,1:T(8,128)S(1)}, f32[64,16]{0,1:T(8,128)S(1)}, f32[64,16,128]{2,0,1:T(8,128)S(1)}) %tuple.130, (s32[256]{0:T(256)S(1)}, s32[256]{0:T(256)S(1)}, s32[256]{0:T(256)S(1)}, ...), branch_computations={%region_19.19_spmd, %region_20.22_spmd} | conditional | flops 137023488 | bytes 5892640 | solution.py:80
  76.6 1.4 pad_maximum_fusion.10
  79.5 1.0 constant_dynamic-slice_fusion.2
  80.6 1.7 fusion.81
  82.3 0.7 and_reduce_fusion.5
  83.7 1.8 conditional.11
  86.0 1.9 %conditional.10 = ((f32[64,16]{0,1:T(8,128)S(1)}, f32[64,16]{0,1:T(8,128)S(1)}, f32[64,16,128]{2,0,1:T(8,128)S(1)})) conditional(s32[]{:T(128)} %convert_element_type.111, (f32[64,16]{0,1:T(8,128)S(1)}, f32[64,16]{0,1:T(8,128)S(1)}, f32[64,16,128]{2,0,1:T(8,128)S(1)}) %tuple.134, (s32[256]{0:T(256)S(1)}, s32[256]{0:T(256)S(1)}, s32[256]{0:T(256)S(1)}, ...), branch_computations={%region_9.9_spmd, %region_10.12_spmd} | conditional | flops 137023488 | bytes 5892640 | solution.py:80
  88.6 1.8 conditional.9
  91.0 1.9 %conditional.8 = ((f32[64,16]{0,1:T(8,128)S(1)}, f32[64,16]{0,1:T(8,128)S(1)}, f32[64,16,128]{2,0,1:T(8,128)S(1)})) conditional(s32[]{:T(128)} %convert_element_type.109, (f32[64,16]{0,1:T(8,128)S(1)}, f32[64,16]{0,1:T(8,128)S(1)}, f32[64,16,128]{2,0,1:T(8,128)S(1)}) %tuple.130, (s32[256]{0:T(256)S(1)}, s32[256]{0:T(256)S(1)}, s32[256]{0:T(256)S(1)}, ...), branch_computations={%region_19.19_spmd, %region_20.22_spmd} | conditional | flops 137023488 | bytes 5892640 | solution.py:80
  93.0 1.4 pad_maximum_fusion.10
  95.9 1.0 constant_dynamic-slice_fusion.2
  97.0 1.7 fusion.81
  98.7 0.7 and_reduce_fusion.5
  100.1 1.8 conditional.11
  102.4 1.9 %conditional.10 = ((f32[64,16]{0,1:T(8,128)S(1)}, f32[64,16]{0,1:T(8,128)S(1)}, f32[64,16,128]{2,0,1:T(8,128)S(1)})) conditional(s32[]{:T(128)} %convert_element_type.111, (f32[64,16]{0,1:T(8,128)S(1)}, f32[64,16]{0,1:T(8,128)S(1)}, f32[64,16,128]{2,0,1:T(8,128)S(1)}) %tuple.134, (s32[256]{0:T(256)S(1)}, s32[256]{0:T(256)S(1)}, s32[256]{0:T(256)S(1)}, ...), branch_computations={%region_9.9_spmd, %region_10.12_spmd} | conditional | flops 137023488 | bytes 5892640 | solution.py:80
  105.0 1.8 conditional.9
  107.4 1.9 %conditional.8 = ((f32[64,16]{0,1:T(8,128)S(1)}, f32[64,16]{0,1:T(8,128)S(1)}, f32[64,16,128]{2,0,1:T(8,128)S(1)})) conditional(s32[]{:T(128)} %convert_element_type.109, (f32[64,16]{0,1:T(8,128)S(1)}, f32[64,16]{0,1:T(8,128)S(1)}, f32[64,16,128]{2,0,1:T(8,128)S(1)}) %tuple.130, (s32[256]{0:T(256)S(1)}, s32[256]{0:T(256)S(1)}, s32[256]{0:T(256)S(1)}, ...), branch_computations={%region_19.19_spmd, %region_20.22_spmd} | conditional | flops 137023488 | bytes 5892640 | solution.py:80
  109.4 1.4 pad_maximum_fusion.10
  112.3 1.0 constant_dynamic-slice_fusion.2
  113.4 1.7 fusion.81
  115.1 0.7 and_reduce_fusion.5
  116.5 1.8 conditional.11
  118.8 1.9 %conditional.10 = ((f32[64,16]{0,1:T(8,128)S(1)}, f32[64,16]{0,1:T(8,128)S(1)}, f32[64,16,128]{2,0,1:T(8,128)S(1)})) conditional(s32[]{:T(128)} %convert_element_type.111, (f32[64,16]{0,1:T(8,128)S(1)}, f32[64,16]{0,1:T(8,128)S(1)}, f32[64,16,128]{2,0,1:T(8,128)S(1)}) %tuple.134, (s32[256]{0:T(256)S(1)}, s32[256]{0:T(256)S(1)}, s32[256]{0:T(256)S(1)}, ...), branch_computations={%region_9.9_spmd, %region_10.12_spmd} | conditional | flops 137023488 | bytes 5892640 | solution.py:80
  121.4 1.8 conditional.9
  123.8 1.9 %conditional.8 = ((f32[64,16]{0,1:T(8,128)S(1)}, f32[64,16]{0,1:T(8,128)S(1)}, f32[64,16,128]{2,0,1:T(8,128)S(1)})) conditional(s32[]{:T(128)} %convert_element_type.109, (f32[64,16]{0,1:T(8,128)S(1)}, f32[64,16]{0,1:T(8,128)S(1)}, f32[64,16,128]{2,0,1:T(8,128)S(1)}) %tuple.130, (s32[256]{0:T(256)S(1)}, s32[256]{0:T(256)S(1)}, s32[256]{0:T(256)S(1)}, ...), branch_computations={%region_19.19_spmd, %region_20.22_spmd} | conditional | flops 137023488 | bytes 5892640 | solution.py:80
  125.8 1.4 pad_maximum_fusion.10
  128.7 1.0 constant_dynamic-slice_fusion.2
  129.8 1.7 fusion.81
  131.5 0.7 and_reduce_fusion.5
  132.9 1.8 conditional.11
  135.2 1.9 %conditional.10 = ((f32[64,16]{0,1:T(8,128)S(1)}, f32[64,16]{0,1:T(8,128)S(1)}, f32[64,16,128]{2,0,1:T(8,128)S(1)})) conditional(s32[]{:T(128)} %convert_element_type.111, (f32[64,16]{0,1:T(8,128)S(1)}, f32[64,16]{0,1:T(8,128)S(1)}, f32[64,16,128]{2,0,1:T(8,128)S(1)}) %tuple.134, (s32[256]{0:T(256)S(1)}, s32[256]{0:T(256)S(1)}, s32[256]{0:T(256)S(1)}, ...), branch_computations={%region_9.9_spmd, %region_10.12_spmd} | conditional | flops 137023488 | bytes 5892640 | solution.py:80
  137.8 1.8 conditional.9
  140.2 1.9 %conditional.8 = ((f32[64,16]{0,1:T(8,128)S(1)}, f32[64,16]{0,1:T(8,128)S(1)}, f32[64,16,128]{2,0,1:T(8,128)S(1)})) conditional(s32[]{:T(128)} %convert_element_type.109, (f32[64,16]{0,1:T(8,128)S(1)}, f32[64,16]{0,1:T(8,128)S(1)}, f32[64,16,128]{2,0,1:T(8,128)S(1)}) %tuple.130, (s32[256]{0:T(256)S(1)}, s32[256]{0:T(256)S(1)}, s32[256]{0:T(256)S(1)}, ...), branch_computations={%region_19.19_spmd, %region_20.22_spmd} | conditional | flops 137023488 | bytes 5892640 | solution.py:80
  142.2 1.4 pad_maximum_fusion.10
  145.1 1.0 constant_dynamic-slice_fusion.2
  146.2 1.7 fusion.81
  147.9 0.7 and_reduce_fusion.5
  151.1 1.4 pad_maximum_fusion.10
  152.7 1.9 %divide_convert_fusion = bf16[256,16,128]{2,0,1:T(8,128)(2,1)S(1)} fusion(f32[256,16,128]{2,0,1:T(8,128)} %get-tuple-element.329, f32[256,16]{0,1:T(8,128)S(1)} %get-tuple-element.330), kind=kLoop, calls=%fused_computation.104 | loop fusion | flops 1048576 | bytes 3162112 | tf_op jit(solution)/shard_map/convert_element_type | solution.py:117
  154.6 0.7 copy.52
  155.8 20.3 %all_to_all.16 = bf16[4,64,2048]{2,1,0:T(8,128)(2,1)S(1)} all-to-all(bf16[4,64,2048]{2,1,0:T(8,128)(2,1)S(1)} %convert_element_type.90), channel_id=1, replica_groups=mesh['srv'=8,'head'=4] {'head'}, dimensions={0} | all-to-all | bytes 2097152 | tf_op jit(solution)/shard_map/all_to_all | solution.py:142
  176.1 1.0 copy.81
  (250 shorter events, 47.5 us)
Async XLA Ops:
  6.5 3.6 %copy-start = (bf16[256,2048]{1,0:T(8,128)(2,1)S(1)}, bf16[256,2048]{1,0:T(8,128)(2,1)}, u32[]{:S(2)}) copy-start(bf16[256,2048]{1,0:T(8,128)(2,1)} %param.13) | copy-start | bytes 3145732
  6.5 31.9 %all-gather.2.cloned.1.call-start = ((), (), s32[]{:S(2)}) async-start(), calls=%async_computation.1 | async-start | bytes 2359296 | tf_op jit(solution)/shard_map/all_gather | solution.py:107
Sparse Core Ops, SparseCore 0:
  10.0 28.3 all-gather.1
where the time goes:
time: 185 us; the launch traced here: 184 us
  other arithmetic  46.3 us (25%)
  local copies, waits for them, and re-layouts  38.3 us (21%)
  loops' own time  26.1 us (14%)
  waiting for transfers between devices  25 us (14%)
  blocking collectives  20.3 us (11%)
  matrix products  14.5 us (8%)
  between operations  13.5 us (7%)
    all_gather x1, waiting for transfers between devices, attend(): kv_piece = lax.all_gather(packed_pair, 'srv', axis=0, tiled=True)  25 us
    another operation x1, loops' own time, attend(): lax.scan(one_step, running, (shards, jnp.arange(shard_count, dtype=jnp.in...  24.9 us
    all_to_all x1, blocking collectives, body(): lax.all_to_all(result, 'head', split_axis=0, concat_axis=1, tiled=True)  20.3 us
    dynamic_slice x24, local copies, waits for them, and re-layouts, attend(): lax.scan(one_step, running, (shards, jnp.arange(shard_count, dtype=jnp.in...  13.5 us
    slice x8, local copies, waits for them, and re-layouts, add_shard(): state[2][row_slice]  13.3 us
    concatenate x8, other arithmetic, add_shard(): jnp.concatenate([item[2] for item in updated], axis=0)  11.5 us
    add x20, other arithmetic, merge_shard(): run_acc * old_factor[..., None] + part_value * new_factor[..., None]  10.1 us
    reduce_sum x20, other arithmetic, merge_shard(): shard_total = jnp.sum(weights, axis=3)  8.24 us
  transfers between devices with their start and end apart: 1, of which 1 were waited for; matrix products, arithmetic and copies ran while one was open for 2% of the time, Pallas kernels for 0%

commit v1 on v0

--- a/solution.py
+++ b/solution.py
@@ -139,7 +139,10 @@
     packed_pair = packed_pair.reshape(tok_rows, 2 * kv_local * HEAD_SIZE)
     query_flat = query_rotated.reshape(tok_rows, query_width)
     result = attend(query_flat, row_ids, starts, packed_pair, tok_rows, kv_local)
-    return lax.all_to_all(result, "head", split_axis=0, concat_axis=1, tiled=True)
+    return jnp.concatenate(
+        lax.all_to_all(jnp.stack(jnp.split(result, lax.axis_size("head"), axis=0)), "head", 0, 0),
+        axis=1,
+    )
 
 
 def solution(mesh):

time: 185 us -> 187 us (1.011)
  no operation moved by 1% of the time
where the time goes in v1:
time: 187 us; the launch traced here: 186 us
  other arithmetic  46.7 us (25%)
  local copies, waits for them, and re-layouts  39.2 us (21%)
  loops' own time  26.2 us (14%)
  waiting for transfers between devices  25.1 us (13%)
  blocking collectives  20.3 us (11%)
  matrix products  14.5 us (8%)
  between operations  13.6 us (7%)
    all_gather x1, waiting for transfers between devices, attend(): kv_piece = lax.all_gather(packed_pair, 'srv', axis=0, tiled=True)  25.1 us
    another operation x1, loops' own time, attend(): lax.scan(one_step, running, (shards, jnp.arange(shard_count, dtype=jnp.in...  24.9 us
    all_to_all x1, blocking collectives, body(): lax.all_to_all(jnp.stack(jnp.split(result, lax.axis_size('head'), axis=0)...  20.3 us
    slice x8, local copies, waits for them, and re-layouts, add_shard(): state[2][row_slice]  14.1 us
    dynamic_slice x24, local copies, waits for them, and re-layouts, attend(): lax.scan(one_step, running, (shards, jnp.arange(shard_count, dtype=jnp.in...  13.5 us
    concatenate x8, other arithmetic, add_shard(): jnp.concatenate([item[2] for item in updated], axis=0)  11.9 us
    add x20, other arithmetic, merge_shard(): run_acc * old_factor[..., None] + part_value * new_factor[..., None]  10.1 us
    reduce_sum x20, other arithmetic, merge_shard(): shard_total = jnp.sum(weights, axis=3)  8.24 us
  transfers between devices with their start and end apart: 1, of which 1 were waited for; matrix products, arithmetic and copies ran while one was open for 2% of the time, Pallas kernels for 0%

profile of v1, /device:TPU:6, one launch (start us, length us, event | category | flops | bytes accessed | tf_op | source)
XLA Modules:
  0.0 185.6 jit_solution(15930331983388430414)
XLA Ops:
  6.6 0.9 reduce-window.8
  7.6 1.0 slice_convert_fusion
  9.2 0.7 pad_maximum_fusion.5
  10.8 0.7 fusion.77
  11.4 1.4 subtract_convert_fusion
  13.4 25.1 %all-gather.2.cloned.1.call-done = bf16[2048,512]{0,1:T(8,128)(2,1)} async-done(((bf16[256,512]{0,1:T(8,128)(2,1)}), bf16[2048,512]{0,1:T(8,128)(2,1)}) %all-gather.2.cloned.1.call-update) | async-done | bytes 2097168 | tf_op jit(solution)/shard_map/all_gather | solution.py:107
  38.4 3.9 %copy.52 = bf16[2048,512]{1,0:T(8,128)(2,1)} copy(bf16[2048,512]{0,1:T(8,128)(2,1)} %all-gather.2.cloned.1.call-done) | data formatting | bytes 4194304 | tf_op jit(solution)/shard_map/all_gather | solution.py:107
  42.4 1.5 broadcast_in_dim.125
  43.9 110.0 %while.18 = (s32[]{:T(128)}, f32[256,16]{0,1:T(8,128)S(1)}, f32[256,16]{0,1:T(8,128)S(1)}, f32[256,16,128]{2,0,1:T(8,128)}, s32[256]{0:T(256)S(1)}, /*index=5*/s...) while((s32[]{:T(128)}, f32[256,16]{0,1:T(8,128)S(1)}, ...), condition=%wide.region_23.24_spmd, body=%wide.region_2.23_spmd.sunk | while | flops 549692672 | bytes 33666752 | solution.py:115
  45.2 1.0 constant_dynamic-slice_fusion.2
  46.4 1.8 fusion.82
  48.1 0.7 and_reduce_fusion.5
  51.3 1.5 pad_maximum_fusion.11
  54.3 1.0 constant_dynamic-slice_fusion.2
  55.4 1.8 fusion.82
  57.2 0.7 and_reduce_fusion.5
  60.4 1.5 pad_maximum_fusion.11
  63.4 1.0 constant_dynamic-slice_fusion.2
  64.5 1.8 fusion.82
  66.3 0.7 and_reduce_fusion.5
  67.7 1.8 conditional.11
  70.0 1.9 %conditional.10 = ((f32[64,16]{0,1:T(8,128)S(1)}, f32[64,16]{0,1:T(8,128)S(1)}, f32[64,16,128]{2,0,1:T(8,128)S(1)})) conditional(s32[]{:T(128)} %convert_element_type.107, (f32[64,16]{0,1:T(8,128)S(1)}, f32[64,16]{0,1:T(8,128)S(1)}, f32[64,16,128]{2,0,1:T(8,128)S(1)}) %tuple.137, (s32[256]{0:T(256)S(1)}, s32[256]{0:T(256)S(1)}, s32[256]{0:T(256)S(1)}, ...), branch_computations={%region_9.9_spmd, %region_10.12_spmd} | conditional | flops 137023488 | bytes 5892640 | solution.py:80
  72.6 1.8 conditional.9
  75.0 1.9 %conditional.8 = ((f32[64,16]{0,1:T(8,128)S(1)}, f32[64,16]{0,1:T(8,128)S(1)}, f32[64,16,128]{2,0,1:T(8,128)S(1)})) conditional(s32[]{:T(128)} %convert_element_type.105, (f32[64,16]{0,1:T(8,128)S(1)}, f32[64,16]{0,1:T(8,128)S(1)}, f32[64,16,128]{2,0,1:T(8,128)S(1)}) %tuple.133, (s32[256]{0:T(256)S(1)}, s32[256]{0:T(256)S(1)}, s32[256]{0:T(256)S(1)}, ...), branch_computations={%region_19.19_spmd, %region_20.22_spmd} | conditional | flops 137023488 | bytes 5892640 | solution.py:80
  77.0 1.5 pad_maximum_fusion.11
  79.9 1.0 constant_dynamic-slice_fusion.2
  81.1 1.8 fusion.82
  82.9 0.7 and_reduce_fusion.5
  84.2 1.8 conditional.11
  86.6 1.9 %conditional.10 = ((f32[64,16]{0,1:T(8,128)S(1)}, f32[64,16]{0,1:T(8,128)S(1)}, f32[64,16,128]{2,0,1:T(8,128)S(1)})) conditional(s32[]{:T(128)} %convert_element_type.107, (f32[64,16]{0,1:T(8,128)S(1)}, f32[64,16]{0,1:T(8,128)S(1)}, f32[64,16,128]{2,0,1:T(8,128)S(1)}) %tuple.137, (s32[256]{0:T(256)S(1)}, s32[256]{0:T(256)S(1)}, s32[256]{0:T(256)S(1)}, ...), branch_computations={%region_9.9_spmd, %region_10.12_spmd} | conditional | flops 137023488 | bytes 5892640 | solution.py:80
  89.2 1.8 conditional.9
  91.6 1.9 %conditional.8 = ((f32[64,16]{0,1:T(8,128)S(1)}, f32[64,16]{0,1:T(8,128)S(1)}, f32[64,16,128]{2,0,1:T(8,128)S(1)})) conditional(s32[]{:T(128)} %convert_element_type.105, (f32[64,16]{0,1:T(8,128)S(1)}, f32[64,16]{0,1:T(8,128)S(1)}, f32[64,16,128]{2,0,1:T(8,128)S(1)}) %tuple.133, (s32[256]{0:T(256)S(1)}, s32[256]{0:T(256)S(1)}, s32[256]{0:T(256)S(1)}, ...), branch_computations={%region_19.19_spmd, %region_20.22_spmd} | conditional | flops 137023488 | bytes 5892640 | solution.py:80
  93.5 1.5 pad_maximum_fusion.11
  96.5 1.0 constant_dynamic-slice_fusion.2
  97.6 1.8 fusion.82
  99.4 0.7 and_reduce_fusion.5
  100.8 1.8 conditional.11
  103.1 1.9 %conditional.10 = ((f32[64,16]{0,1:T(8,128)S(1)}, f32[64,16]{0,1:T(8,128)S(1)}, f32[64,16,128]{2,0,1:T(8,128)S(1)})) conditional(s32[]{:T(128)} %convert_element_type.107, (f32[64,16]{0,1:T(8,128)S(1)}, f32[64,16]{0,1:T(8,128)S(1)}, f32[64,16,128]{2,0,1:T(8,128)S(1)}) %tuple.137, (s32[256]{0:T(256)S(1)}, s32[256]{0:T(256)S(1)}, s32[256]{0:T(256)S(1)}, ...), branch_computations={%region_9.9_spmd, %region_10.12_spmd} | conditional | flops 137023488 | bytes 5892640 | solution.py:80
  105.7 1.8 conditional.9
  108.1 1.9 %conditional.8 = ((f32[64,16]{0,1:T(8,128)S(1)}, f32[64,16]{0,1:T(8,128)S(1)}, f32[64,16,128]{2,0,1:T(8,128)S(1)})) conditional(s32[]{:T(128)} %convert_element_type.105, (f32[64,16]{0,1:T(8,128)S(1)}, f32[64,16]{0,1:T(8,128)S(1)}, f32[64,16,128]{2,0,1:T(8,128)S(1)}) %tuple.133, (s32[256]{0:T(256)S(1)}, s32[256]{0:T(256)S(1)}, s32[256]{0:T(256)S(1)}, ...), branch_computations={%region_19.19_spmd, %region_20.22_spmd} | conditional | flops 137023488 | bytes 5892640 | solution.py:80
  110.1 1.5 pad_maximum_fusion.11
  113.1 1.0 constant_dynamic-slice_fusion.2
  114.2 1.8 fusion.82
  116.0 0.7 and_reduce_fusion.5
  117.3 1.8 conditional.11
  119.7 1.9 %conditional.10 = ((f32[64,16]{0,1:T(8,128)S(1)}, f32[64,16]{0,1:T(8,128)S(1)}, f32[64,16,128]{2,0,1:T(8,128)S(1)})) conditional(s32[]{:T(128)} %convert_element_type.107, (f32[64,16]{0,1:T(8,128)S(1)}, f32[64,16]{0,1:T(8,128)S(1)}, f32[64,16,128]{2,0,1:T(8,128)S(1)}) %tuple.137, (s32[256]{0:T(256)S(1)}, s32[256]{0:T(256)S(1)}, s32[256]{0:T(256)S(1)}, ...), branch_computations={%region_9.9_spmd, %region_10.12_spmd} | conditional | flops 137023488 | bytes 5892640 | solution.py:80
  122.3 1.8 conditional.9
  124.7 1.9 %conditional.8 = ((f32[64,16]{0,1:T(8,128)S(1)}, f32[64,16]{0,1:T(8,128)S(1)}, f32[64,16,128]{2,0,1:T(8,128)S(1)})) conditional(s32[]{:T(128)} %convert_element_type.105, (f32[64,16]{0,1:T(8,128)S(1)}, f32[64,16]{0,1:T(8,128)S(1)}, f32[64,16,128]{2,0,1:T(8,128)S(1)}) %tuple.133, (s32[256]{0:T(256)S(1)}, s32[256]{0:T(256)S(1)}, s32[256]{0:T(256)S(1)}, ...), branch_computations={%region_19.19_spmd, %region_20.22_spmd} | conditional | flops 137023488 | bytes 5892640 | solution.py:80
  126.6 1.5 pad_maximum_fusion.11
  129.6 1.0 constant_dynamic-slice_fusion.2
  130.8 1.8 fusion.82
  132.5 0.7 and_reduce_fusion.5
  133.9 1.8 conditional.11
  136.3 1.9 %conditional.10 = ((f32[64,16]{0,1:T(8,128)S(1)}, f32[64,16]{0,1:T(8,128)S(1)}, f32[64,16,128]{2,0,1:T(8,128)S(1)})) conditional(s32[]{:T(128)} %convert_element_type.107, (f32[64,16]{0,1:T(8,128)S(1)}, f32[64,16]{0,1:T(8,128)S(1)}, f32[64,16,128]{2,0,1:T(8,128)S(1)}) %tuple.137, (s32[256]{0:T(256)S(1)}, s32[256]{0:T(256)S(1)}, s32[256]{0:T(256)S(1)}, ...), branch_computations={%region_9.9_spmd, %region_10.12_spmd} | conditional | flops 137023488 | bytes 5892640 | solution.py:80
  138.8 1.8 conditional.9
  141.3 1.9 %conditional.8 = ((f32[64,16]{0,1:T(8,128)S(1)}, f32[64,16]{0,1:T(8,128)S(1)}, f32[64,16,128]{2,0,1:T(8,128)S(1)})) conditional(s32[]{:T(128)} %convert_element_type.105, (f32[64,16]{0,1:T(8,128)S(1)}, f32[64,16]{0,1:T(8,128)S(1)}, f32[64,16,128]{2,0,1:T(8,128)S(1)}) %tuple.133, (s32[256]{0:T(256)S(1)}, s32[256]{0:T(256)S(1)}, s32[256]{0:T(256)S(1)}, ...), branch_computations={%region_19.19_spmd, %region_20.22_spmd} | conditional | flops 137023488 | bytes 5892640 | solution.py:80
  143.2 1.5 pad_maximum_fusion.11
  146.2 1.0 constant_dynamic-slice_fusion.2
  147.3 1.8 fusion.82
  149.1 0.7 and_reduce_fusion.5
  152.3 1.5 pad_maximum_fusion.11
  153.9 1.9 %divide_convert_fusion = bf16[256,16,128]{2,0,1:T(8,128)(2,1)S(1)} fusion(f32[256,16,128]{2,0,1:T(8,128)} %get-tuple-element.329, f32[256,16]{0,1:T(8,128)S(1)} %get-tuple-element.330), kind=kLoop, calls=%fused_computation.104 | loop fusion | flops 1048576 | bytes 3162112 | tf_op jit(solution)/shard_map/convert_element_type | solution.py:117
  157.3 20.3 %all_to_all.5 = bf16[4,64,2048]{2,1,0:T(8,128)(2,1)S(1)} all-to-all(bf16[4,64,2048]{2,1,0:T(8,128)(2,1)S(1)} %pad_maximum_fusion.4), channel_id=1, replica_groups=mesh['srv'=8,'head'=4] {'head'}, dimensions={0} | all-to-all | bytes 2097152 | tf_op jit(solution)/shard_map/all_to_all | solution.py:143
  177.6 1.1 copy.90
  (258 shorter events, 47.7 us)
Async XLA Ops:
  6.5 3.6 %copy-start = (bf16[256,2048]{1,0:T(8,128)(2,1)S(1)}, bf16[256,2048]{1,0:T(8,128)(2,1)}, u32[]{:S(2)}) copy-start(bf16[256,2048]{1,0:T(8,128)(2,1)} %param.13) | copy-start | bytes 3145732
  6.5 31.9 %all-gather.2.cloned.1.call-start = ((), (), s32[]{:S(2)}) async-start(), calls=%async_computation.1 | async-start | bytes 2359296 | tf_op jit(solution)/shard_map/all_gather | solution.py:107
Sparse Core Ops, SparseCore 0:
  10.0 28.3 all-gather.1
